TPU v7x, 32 devices: a whole 2x2x4 slice. The times are simulated.
32 devices in a mesh: scene: 2 (over y), az: 8 (over z, x), rg: 2 (over core).
Axes of the slice: x: 2, y: 2, z: 4, core: 2. Of those that a mesh axis runs over, the one named last changes fastest.
Arguments:
- raw_re: float32 [64, 32768], P('rg', ('scene', 'az')), parts along dimension 1, may hold values from -6 to 6
- raw_im: float32 [64, 32768], P('rg', ('scene', 'az')), parts along dimension 1, may hold values from -6 to 6
- ref_blocks: float32 [16, 64, 64], P(('scene', 'az'), None, 'rg'), parts along dimension 0, may hold values from -3.140625 to 3.140625
- owners: int32 [4], P('scene'), parts along dimension 0, may hold values from 0 to 7, as said below
- offsets: int32 [4], P('rg'), may hold values from -8 to 8
- taps: float32 [64, 8], P('rg'), may hold values from -3 to 3
Outputs:
- image_re: float32 [64, 32768], P('rg', ('scene', 'az')), parts along dimension 1
- image_im: float32 [64, 32768], P('rg', ('scene', 'az')), parts along dimension 1
There are 2 independent parts, one for each index of `scene`. A program takes and returns all parts, laid end to end along the dimension named above; an argument that names none is the same for every part. Nothing has to cross between parts.
Inputs may be any that keep to these rules, and one draw needn't show every extreme that they name: The two sub-apertures have different owners.
All inputs are finite; a program needn't handle non-finite values.
Results may differ from a plain program's by a relative error of at most 0.00014.
Values sent between devices are 32-bit elements; how exact they have to be, the bound alone decides.
A program may use at most 64 MiB of HBM per device.

v0:
```python
import functools
import math

import jax
import jax.numpy as jnp
import ml_dtypes
import numpy as np
from jax import lax
from jax.experimental import pallas as pl
from jax.experimental.pallas import tpu as pltpu
from jax.sharding import PartitionSpec as P

SPLIT = 4
TAPS = 8
REACH = 8
BLOCK = 16


PRECISE = lax.Precision.HIGHEST
PHASE_GAIN = 50.0


def partner_2(value, axis, stride):
    return lax.ppermute(value, axis, [(i, i ^ 1 << stride) for i in range(lax.axis_size(axis))])


def from_root(block, axis, source):
    block = jnp.where(lax.axis_index(axis) == source, block, jnp.zeros_like(block))
    return lax.psum(block, axis)


def padded_2(value, sides, width):
    for axis, dim in sides:
        size, length = (lax.axis_size(axis), value.shape[dim])
        up = [(i, (i + 1) % size) for i in range(size - 1)]
        down = [(j, i) for i, j in up]
        last = lax.slice_in_dim(value, length - width, length, axis=dim)
        initial = lax.slice_in_dim(value, 0, width, axis=dim)
        before = lax.ppermute(last, axis, up)
        after = lax.ppermute(initial, axis, down)
        value = jnp.concatenate([before, value, after], axis=dim)
    return value


def angles(numerator, denominator, sign_value):
    return sign_value * 2.0 * math.pi * numerator.astype(jnp.float32) / denominator


def rotate(signal, cosine, sine_part):
    real_part = signal[0] * cosine - signal[1] * sine_part
    imag_part = signal[0] * sine_part + signal[1] * cosine
    return jnp.stack([real_part, imag_part])


def dft_table(length_n, sign_value):
    counter = jnp.arange(length_n, dtype=jnp.int32)
    turn_count = counter[:, None] * counter[None, :] % length_n
    angle_set = angles(turn_count, length_n, sign_value)
    return (jnp.cos(angle_set), jnp.sin(angle_set))


def complex_apply(einsum_form, cosine, sine_part, signal):
    real_part = jnp.einsum(einsum_form, cosine, signal[0], precision=PRECISE) - jnp.einsum(
        einsum_form, sine_part, signal[1], precision=PRECISE
    )
    imag_part = jnp.einsum(einsum_form, cosine, signal[1], precision=PRECISE) + jnp.einsum(
        einsum_form, sine_part, signal[0], precision=PRECISE
    )
    return jnp.stack([real_part, imag_part])


def local_dft(signal, sign_value):
    rg_cols = signal.shape[1]
    az_rows = signal.shape[2]
    inner_len = az_rows // SPLIT
    shaped = signal.reshape(2, rg_cols, SPLIT, inner_len)
    first_cos, first_sin = dft_table(SPLIT, sign_value)
    first_pass = complex_apply("aj,cjk->cak", first_cos, first_sin, shaped)
    outer_idx = jnp.arange(SPLIT, dtype=jnp.int32)
    inner_idx = jnp.arange(inner_len, dtype=jnp.int32)
    twist = angles(outer_idx[:, None] * inner_idx[None, :] % az_rows, az_rows, sign_value)
    first_pass = rotate(first_pass, jnp.cos(twist)[None, :, :], jnp.sin(twist)[None, :, :])
    second_cos, second_sin = dft_table(inner_len, sign_value)
    second_pass = complex_apply("bk,cak->cba", second_cos, second_sin, first_pass)
    return second_pass.reshape(2, rg_cols, az_rows)


def butterfly_down(signal, az_place, bit_count):
    for bit_num in reversed(range(bit_count)):
        half_span = 1 << bit_num
        partner = partner_2(signal, "az", bit_num)
        is_upper = az_place >> bit_num & 1 == 1
        angle_set = angles(az_place % half_span, 2 * half_span, -1.0)
        difference = rotate(partner - signal, jnp.cos(angle_set), jnp.sin(angle_set))
        signal = jnp.where(is_upper, difference, signal + partner)
    return signal


def butterfly_up(signal, az_place, bit_count):
    for bit_num in range(bit_count):
        half_span = 1 << bit_num
        partner = partner_2(signal, "az", bit_num)
        is_upper = az_place >> bit_num & 1 == 1
        angle_set = angles(az_place % half_span, 2 * half_span, 1.0)
        cosine = jnp.cos(angle_set)
        sine_part = jnp.sin(angle_set)
        lower_new = (signal + rotate(partner, cosine, sine_part)) * 0.5
        upper_new = (partner - rotate(signal, cosine, sine_part)) * 0.5
        signal = jnp.where(is_upper, upper_new, lower_new)
    return signal


def shards(raw_re, raw_im, ref_blocks, owners, offsets, taps):
    rg_cols = raw_re.shape[0]
    az_rows = raw_re.shape[1]
    az_count = lax.axis_size("az")
    az_place = lax.axis_index("az")
    bit_count = az_count.bit_length() - 1
    az_total = az_rows * az_count
    rg_total = rg_cols * lax.axis_size("rg")
    own_block = ref_blocks[0]
    lower_ref = from_root(own_block, "az", owners[0])
    upper_ref = from_root(own_block, "az", owners[1])
    signal = jnp.stack([raw_re, raw_im])
    signal = butterfly_down(signal, az_place, bit_count)
    column = jnp.zeros((), jnp.int32)
    for bit_num in range(bit_count):
        column = column + ((az_place >> bit_num & 1) << bit_count - 1 - bit_num)
    row_index = jnp.arange(az_rows, dtype=jnp.int32)
    twist = angles(row_index * column % az_total, az_total, -1.0)
    signal = rotate(signal, jnp.cos(twist)[None, :], jnp.sin(twist)[None, :])
    signal = local_dft(signal, -1.0)
    frequency = column + az_count * row_index
    signed = (frequency + az_total // 2) % az_total - az_total // 2
    az_freq = signed.astype(jnp.float32) / az_total
    rg_index = lax.axis_index("rg") * rg_cols + jnp.arange(rg_cols, dtype=jnp.int32)
    rg_freq = (rg_index.astype(jnp.float32) + 0.5) / (2 * rg_total) - 0.25
    model_phase = PHASE_GAIN * jnp.sqrt((1.0 + rg_freq)[:, None] ** 2 - az_freq[None, :] ** 2)
    ref_rows = own_block.shape[0]
    coarse = frequency * ref_rows // az_total
    slot_index = jnp.where(signed >= 0, ref_rows + coarse, coarse)
    one_hot = (jnp.arange(2 * ref_rows, dtype=jnp.int32)[:, None] == slot_index[None, :]).astype(
        jnp.float32
    )
    both_refs = jnp.concatenate([lower_ref, upper_ref], axis=0)
    picked = jnp.dot(both_refs.T, one_hot, precision=PRECISE)
    phase_all = model_phase + picked
    signal = rotate(signal, jnp.cos(phase_all), jnp.sin(phase_all))
    rim_width = REACH + TAPS // 2
    padded = padded_2(signal, (("rg", 1),), rim_width)
    offset_cols = jnp.repeat(offsets, BLOCK)
    local_cols = jnp.arange(rg_cols, dtype=jnp.int32)
    tap_index = jnp.arange(TAPS, dtype=jnp.int32)
    target = local_cols[:, None] + rim_width + offset_cols[:, None] + tap_index[None, :] - TAPS // 2
    padded_index = jnp.arange(rg_cols + 2 * rim_width, dtype=jnp.int32)
    hits = (padded_index[:, None, None] == target[None, :, :]).astype(jnp.float32)
    band_matrix = jnp.sum(hits * taps[None, :, :], axis=2)
    signal = jnp.einsum("zma,mi->zia", padded, band_matrix, precision=PRECISE)
    signal = local_dft(signal, 1.0) / az_rows
    twist_back = angles(row_index * column % az_total, az_total, 1.0)
    signal = rotate(signal, jnp.cos(twist_back)[None, :], jnp.sin(twist_back)[None, :])
    signal = butterfly_up(signal, az_place, bit_count)
    return (signal[0], signal[1])


LANES = 128
MESH = pl.DeviceIdType.MESH
RIM = REACH + TAPS // 2
TWO_PI_HI = 6.28125
TWO_PI_LO = 2.0 * math.pi - TWO_PI_HI


def split_np(matrix):
    high = matrix.astype(np.float32).astype(ml_dtypes.bfloat16)
    low = (matrix - high.astype(np.float64)).astype(np.float32).astype(ml_dtypes.bfloat16)
    return np.stack([high, low])


def tables(az_count):
    inner = LANES // az_count
    grid = np.arange(LANES)
    angle = 2.0 * np.pi * (np.outer(grid, grid) % LANES) / LANES
    cos, sin = np.cos(angle), -np.sin(angle)
    forward = [[cos, -sin], [sin, cos]]
    inverse = [[cos, sin], [-sin, cos]]
    order = np.arange(2 * LANES).reshape(2, az_count, inner).transpose(1, 0, 2).reshape(-1)
    left_in = np.block(forward)[:, order]
    right_in = np.block([[forward[o][c].T for o in range(2)] for c in range(2)])
    right_out = np.block([[inverse[o][c].T for o in range(2)] for c in range(2)])
    left_out = np.block(inverse)[order, :] / (LANES * LANES)
    matrices = np.stack([split_np(m) for m in (left_in, right_in, right_out, left_out)])
    turn = 2.0 * np.pi * np.outer(grid, grid) / (LANES * LANES)
    twiddle = np.stack([np.cos(turn), -np.sin(turn)]).astype(np.float32)
    return matrices, twiddle


def split(value):
    high = value.astype(jnp.bfloat16)
    low = (value - high.astype(jnp.float32)).astype(jnp.bfloat16)
    return high, low


def dot(a, b):
    return jnp.dot(a, b, preferred_element_type=jnp.float32)


def left_apply(table, value):
    high, low = split(value)
    return dot(table[0], high) + (dot(table[0], low) + dot(table[1], high))


def right_apply(value, table):
    high, low = split(value)
    return dot(high, table[0]) + (dot(low, table[0]) + dot(high, table[1]))


def cos_sin(phase):
    turns = jnp.floor(phase * (0.5 / math.pi) + 0.5)
    rest = (phase - turns * TWO_PI_HI) - turns * TWO_PI_LO
    half = rest * 0.5
    square = half * half
    sine = jnp.full_like(square, -1.0 / math.factorial(11))
    for power in (9, 7, 5, 3, 1):
        sine = sine * square + (-1.0) ** (power // 2) / math.factorial(power)
    sine = sine * half
    cosine = jnp.full_like(square, 1.0 / math.factorial(12))
    for power in (10, 8, 6, 4, 2, 0):
        cosine = cosine * square + (-1.0) ** (power // 2) / math.factorial(power)
    return 1.0 - 2.0 * sine * sine, 2.0 * sine * cosine


def focus_kernel(
    az_count,
    raw_re,
    raw_im,
    refs,
    owners,
    offsets,
    taps,
    matrices_hbm,
    twiddle_hbm,
    out_re,
    out_im,
    matrices,
    twiddle,
    outgoing,
    incoming,
    ref_out,
    ref_in,
    filt,
    focused,
    band,
    weigh,
    const_sem,
    ref_send,
    ref_recv,
    in_send,
    in_recv,
    back_send,
    back_recv,
    rim_send,
    rim_recv,
):
    rows = raw_re.shape[0]
    inner = raw_re.shape[1] // LANES
    piece = 2 * inner
    steps = rows // az_count
    depth = band.shape[0] // piece
    me = lax.axis_index("az")
    core = lax.axis_index("rg")
    peers = [lax.rem(me + s, az_count) for s in range(1, az_count)]
    sources = [lax.rem(me + az_count - s, az_count) for s in range(1, az_count)]
    sibling = 1 - core

    barrier = pltpu.get_barrier_semaphore()
    for peer in peers:
        pl.semaphore_signal(barrier, inc=1, device_id={"az": peer}, device_id_type=MESH)
    pl.semaphore_signal(barrier, inc=1, device_id={"rg": sibling}, device_id_type=MESH)
    load_matrices = pltpu.make_async_copy(matrices_hbm, matrices, const_sem.at[0])
    load_twiddle = pltpu.make_async_copy(twiddle_hbm, twiddle, const_sem.at[1])
    load_matrices.start()
    load_twiddle.start()

    groups = [s + (1 - core) * (steps - 1 - 2 * s) for s in range(steps)]

    def at(start, count):
        return pl.ds(start * piece if isinstance(start, int) else pl.multiple_of(start * piece, piece), count * piece)

    for comp, raw in enumerate((raw_re, raw_im)):
        for i in range(inner):
            outgoing[pl.ds(comp * inner + i, rows, stride=piece), :] = raw[:, i * LANES : (i + 1) * LANES]

    ref_rows = refs.shape[1]
    slot = lax.broadcasted_iota(jnp.int32, (depth, rows), 0)
    target = lax.broadcasted_iota(jnp.int32, (depth, rows), 1)
    target_block = target // BLOCK
    for block in range(rows // BLOCK):
        target = jnp.where(target_block == block, target + offsets[block], target)
    weights = jnp.zeros((depth, rows), jnp.float32)
    for tap in range(TAPS):
        weights = weights + jnp.where(slot == target + (RIM + tap - TAPS // 2), taps[tap : tap + 1, :], 0.0)
    high, low = split(weights.T)
    weigh[...] = jnp.concatenate([high, high, low], axis=1)
    coarse = lax.broadcasted_iota(jnp.int32, (ref_rows, LANES), 0)
    column = lax.broadcasted_iota(jnp.int32, (ref_rows, LANES), 1)
    spread = (coarse == column // (LANES // ref_rows)).astype(jnp.float32)
    wide = jnp.dot(refs[...], spread, precision=PRECISE, preferred_element_type=jnp.float32)
    ref_out[...] = jnp.zeros_like(ref_out)
    for dest in range(az_count):
        for group in range(steps):
            row = group * az_count + dest
            ref_out[dest, group : group + 1, :] = wide[row : row + 1, :]

    pl.semaphore_wait(barrier, az_count)

    def ref_copy(s, peer, source):
        return pltpu.make_async_remote_copy(
            src_ref=ref_out.at[peer],
            dst_ref=ref_in.at[source],
            send_sem=ref_send.at[s],
            recv_sem=ref_recv.at[source],
            device_id={"az": peer},
            device_id_type=MESH,
        )

    def in_copy(step, s, peer, source):
        return pltpu.make_async_remote_copy(
            src_ref=outgoing.at[at(groups[step] * az_count + peer, 1), :],
            dst_ref=incoming.at[at(groups[step] * az_count + source, 1), :],
            send_sem=in_send.at[step, s],
            recv_sem=in_recv.at[step, source],
            device_id={"az": peer},
            device_id_type=MESH,
        )

    def back_copy(step, s, peer, source):
        return pltpu.make_async_remote_copy(
            src_ref=focused.at[at(groups[step] * az_count + peer, 1), :],
            dst_ref=band.at[at(RIM + groups[step] * az_count + source, 1), :],
            send_sem=back_send.at[step, s],
            recv_sem=back_recv.at[step, source],
            device_id={"az": peer},
            device_id_type=MESH,
        )

    def rim_copy(step):
        count = (az_count, RIM - az_count)[step]
        first = ((rows - az_count, rows - RIM)[step], (0, az_count)[step])
        place = ((RIM - az_count, 0)[step], (RIM + rows, RIM + rows + az_count)[step])
        return pltpu.make_async_remote_copy(
            src_ref=band.at[at(RIM + first[0] * (1 - core) + first[1] * core, count), :],
            dst_ref=band.at[at(place[0] * (1 - core) + place[1] * core, count), :],
            send_sem=rim_send.at[step],
            recv_sem=rim_recv.at[step],
            device_id={"rg": sibling},
            device_id_type=MESH,
        )

    def rim_arrival(step):
        count = (az_count, RIM - az_count)[step]
        place = ((RIM - az_count, 0)[step], (RIM + rows, RIM + rows + az_count)[step])
        return pltpu.make_async_remote_copy(
            src_ref=band.at[at(RIM, count), :],
            dst_ref=band.at[at(place[0] * core + place[1] * (1 - core), count), :],
            send_sem=rim_send.at[step],
            recv_sem=rim_recv.at[step],
            device_id={"rg": sibling},
            device_id_type=MESH,
        )

    for s, peer in enumerate(peers):
        ref_copy(s, peer, me).start()
    for step in range(steps):
        for s, peer in enumerate(peers):
            in_copy(step, s, peer, me).start()

    for group in range(steps):
        own = at(group * az_count + me, 1)
        incoming[own, :] = outgoing[own, :]
    ref_in[me] = ref_out[me]
    band[at((RIM + rows) * core, RIM), :] = jnp.zeros((RIM * piece, LANES), jnp.float32)
    spare = depth - rows - 2 * RIM
    band[at(depth - spare, spare), :] = jnp.zeros((spare * piece, LANES), jnp.float32)

    for s, source in enumerate(sources):
        ref_copy(s, peers[s], source).wait_recv()
    lane = lax.broadcasted_iota(jnp.int32, ref_in.shape[1:], 1)
    picked = jnp.zeros(ref_in.shape[1:], jnp.float32)
    for source in range(az_count):
        wanted = jnp.where(lane < LANES // 2, owners[1], owners[0]) == source
        picked = jnp.where(wanted, ref_in[source], picked)
    az_total = LANES * LANES
    low = lax.broadcasted_iota(jnp.int32, (LANES, LANES), 0)
    high = lax.broadcasted_iota(jnp.int32, (LANES, LANES), 1)
    frequency = low + LANES * high
    signed = jnp.where(frequency >= az_total // 2, frequency - az_total, frequency)
    az_freq = signed.astype(jnp.float32) / az_total
    az_square = az_freq * az_freq
    for group in range(steps):
        index = core * rows + group * az_count + me
        rg_freq = 1.0 + ((index.astype(jnp.float32) + 0.5) * (1.0 / (4 * rows)) - 0.25)
        phase = PHASE_GAIN * jnp.sqrt(rg_freq * rg_freq - az_square) + picked[group : group + 1, :]
        cosine, sine = cos_sin(phase)
        filt[group, 0] = cosine
        filt[group, 1] = sine

    load_matrices.wait()
    load_twiddle.wait()
    for step in range(steps):
        group = groups[step]
        for s, source in enumerate(sources):
            in_copy(step, s, peers[s], source).wait_recv()
        whole = at(group * az_count, az_count)
        value = left_apply((matrices[0, 0], matrices[0, 1]), incoming[whole, :])
        cosine, sine = twiddle[0], twiddle[1]
        real, imag = value[:LANES], value[LANES:]
        value = jnp.concatenate([real * cosine - imag * sine, real * sine + imag * cosine], axis=1)
        value = right_apply(value, (matrices[1, 0], matrices[1, 1]))
        real, imag = value[:, :LANES], value[:, LANES:]
        cosine, sine = filt[group, 0], filt[group, 1]
        value = jnp.concatenate([real * cosine - imag * sine, real * sine + imag * cosine], axis=1)
        value = right_apply(value, (matrices[2, 0], matrices[2, 1]))
        real, imag = value[:, :LANES], value[:, LANES:]
        cosine, sine = twiddle[0], twiddle[1]
        value = jnp.concatenate([real * cosine + imag * sine, imag * cosine - real * sine], axis=0)
        focused[whole, :] = left_apply((matrices[3, 0], matrices[3, 1]), value)
        for s, peer in enumerate(peers):
            back_copy(step, s, peer, me).start()
        band[at(RIM + group * az_count + me, 1), :] = focused[at(group * az_count + me, 1), :]
        if step >= steps - 2:
            early = step - (steps - 2)
            for s, source in enumerate(sources):
                back_copy(early, s, peers[s], source).wait_recv()
            rim_copy(early).start()
    for step in range(2, steps):
        for s, source in enumerate(sources):
            back_copy(step, s, peers[s], source).wait_recv()
    for step in range(2):
        rim_arrival(step).wait_recv()

    weights = weigh[...]
    pair = 2 * LANES
    for comp, out in enumerate((out_re, out_im)):
        for i in range(0, inner, 2):
            value = jnp.concatenate(
                [band[pl.ds(comp * inner + i + j, depth, stride=piece), :] for j in range(2)], axis=1
            )
            high, low = split(value)
            value = dot(weights, jnp.concatenate([high, low, high], axis=0))
            out[:, i * LANES : i * LANES + pair] = value

    for s, peer in enumerate(peers):
        ref_copy(s, peer, me).wait_send()
        for step in range(steps):
            in_copy(step, s, peer, me).wait_send()
            back_copy(step, s, peer, me).wait_send()
    for step in range(2):
        rim_copy(step).wait_send()


def fused_shards(az_count, raw_re, raw_im, ref_blocks, owners, offsets, taps):
    rows, samples = raw_re.shape
    piece = 2 * samples // LANES
    steps = rows // az_count
    depth = -(-(rows + 2 * RIM) // 16) * 16
    matrices, twiddle = tables(az_count)
    vmem = pl.BlockSpec(memory_space=pltpu.VMEM)
    smem = pl.BlockSpec(memory_space=pltpu.SMEM)
    anywhere = pl.BlockSpec(memory_space=pl.ANY)
    dma = pltpu.SemaphoreType.DMA
    flat = pltpu.VMEM((rows * piece, LANES), jnp.float32)
    return pl.pallas_call(
        functools.partial(focus_kernel, az_count),
        out_shape=[jax.ShapeDtypeStruct(raw_re.shape, jnp.float32)] * 2,
        in_specs=[vmem, vmem, vmem, smem, smem, vmem, anywhere, anywhere],
        out_specs=[vmem, vmem],
        scratch_shapes=[
            pltpu.VMEM(matrices.shape, jnp.bfloat16),
            pltpu.VMEM(twiddle.shape, jnp.float32),
            flat,
            flat,
            pltpu.VMEM((az_count, 8, LANES), jnp.float32),
            pltpu.VMEM((az_count, 8, LANES), jnp.float32),
            pltpu.VMEM((steps, 2, LANES, LANES), jnp.float32),
            flat,
            pltpu.VMEM((depth * piece, LANES), jnp.float32),
            pltpu.VMEM((rows, 3 * depth), jnp.bfloat16),
            dma((2,)),
            dma((az_count,)),
            dma((az_count,)),
            dma((steps, az_count)),
            dma((steps, az_count)),
            dma((steps, az_count)),
            dma((steps, az_count)),
            dma((2,)),
            dma((2,)),
        ],
        compiler_params=pltpu.CompilerParams(
            collective_id=0, has_side_effects=True, vmem_limit_bytes=32 * 1024 * 1024
        ),
    )(raw_re, raw_im, ref_blocks[0].T, owners, offsets, taps.T, jnp.asarray(matrices), jnp.asarray(twiddle))


def body_for(mesh):
    az_count, rg_count = mesh.shape["az"], mesh.shape["rg"]

    def body(raw_re, raw_im, ref_blocks, owners, offsets, taps):
        rows, samples = raw_re.shape
        fits = (
            samples * az_count == LANES * LANES
            and az_count == 8
            and rows == 4 * az_count
            and rg_count == 2
            and ref_blocks.shape[1] == 64
        )
        if fits:
            return tuple(fused_shards(az_count, raw_re, raw_im, ref_blocks, owners, offsets, taps))
        return shards(raw_re, raw_im, ref_blocks, owners, offsets, taps)

    return body


def solution(mesh):
    return jax.shard_map(
        body_for(mesh),
        mesh=mesh,
        in_specs=(
            P("rg", ("scene", "az")),
            P("rg", ("scene", "az")),
            P(("scene", "az"), None, "rg"),
            P("scene"),
            P("rg"),
            P("rg", None),
        ),
        out_specs=(P("rg", ("scene", "az")), P("rg", ("scene", "az"))),
        check_vma=False,
    )
```

profile of v0, /device:TPU:0, one launch (start us, length us, event | category | flops | bytes accessed | tf_op | source)
XLA Modules:
  0.0 42.4 jit_solution(10794349384324172803)
XLA Ops:
  0.6 0.0 copy-start.6
  0.6 0.0 copy-start.7
  0.7 0.6 %copy-done.6 = s32[2]{0:T(128)S(1)} copy-done((s32[2]{0:T(128)S(1)}, s32[2]{0:T(128)}, u32[]{:S(2)}) %copy-start.6) | copy-done | bytes 32
  1.3 0.0 copy-done.7
  1.3 0.0 copy-start
  1.3 1.2 %copy-done = bf16[4,2,256,256]{3,2,1,0:T(8,128)(2,1)S(1)} copy-done((bf16[4,2,256,256]{3,2,1,0:T(8,128)(2,1)S(1)}, bf16[4,2,256,256]{3,2,1,0:T(8,128)(2,1)}, u32[]{:S(2)}) %copy-start) | copy-done | bytes 1048600
  2.5 0.0 copy-start.1
  2.5 0.9 %copy-done.1 = f32[32,2048]{1,0:T(8,128)S(1)} copy-done((f32[32,2048]{1,0:T(8,128)S(1)}, f32[32,2048]{1,0:T(8,128)}, u32[]{:S(2)}) %copy-start.1) | copy-done | bytes 262168
  3.5 0.0 copy-start.2
  3.5 0.9 %copy-done.2 = f32[32,2048]{1,0:T(8,128)S(1)} copy-done((f32[32,2048]{1,0:T(8,128)S(1)}, f32[32,2048]{1,0:T(8,128)}, u32[]{:S(2)}) %copy-start.2) | copy-done | bytes 262168
  4.4 0.0 copy-start.3
  4.4 0.9 %copy-done.3 = f32[2,128,128]{2,1,0:T(8,128)S(1)} copy-done((f32[2,128,128]{2,1,0:T(8,128)S(1)}, f32[2,128,128]{2,1,0:T(8,128)}, u32[]{:S(2)}) %copy-start.3) | copy-done | bytes 131096
  5.3 0.0 copy-start.4
  5.3 0.7 %copy-done.4 = f32[1,64,32]{1,2,0:T(8,128)S(1)} copy-done((f32[1,64,32]{1,2,0:T(8,128)S(1)}, f32[1,64,32]{1,2,0:T(8,128)}, u32[]{:S(2)}) %copy-start.4) | copy-done | bytes 8216
  6.1 0.0 copy-start.5
  6.1 0.7 %copy-done.5 = f32[32,8]{0,1:T(8,128)S(1)} copy-done((f32[32,8]{0,1:T(8,128)S(1)}, f32[32,8]{0,1:T(8,128)}, u32[]{:S(2)}) %copy-start.5) | copy-done | bytes 1048
  6.7 34.3 %shard_map.95 = (f32[32,2048]{1,0:T(8,128)S(1)}, f32[32,2048]{1,0:T(8,128)S(1)}) custom-call(f32[32,2048]{1,0:T(8,128)S(1)} %copy-done.1, f32[32,2048]{1,0:T(8,128)S(1)} %copy-done.2, f32[32,64]{1,0:T(8,128)S(1)} %bitcast.4, s32[2]{0:T(128)S(1)} %copy-done.6, s32[2]{0:T(128)S(1)} %copy-done.7, f32[8,32]{1,0:T(8,128)S(1)} %bitcast.5, ...), custom_call_target="tpu_custom_call" | custom-call | tf_op jit(solution)/shard_map/pallas_call | solution.py:472
  41.0 0.7 %copy.12 = f32[32,2048]{1,0:T(8,128)} copy(f32[32,2048]{1,0:T(8,128)S(1)} %get-tuple-element.4) | data formatting | bytes 524288
  41.7 0.7 %copy.13 = f32[32,2048]{1,0:T(8,128)} copy(f32[32,2048]{1,0:T(8,128)S(1)} %get-tuple-element.5) | data formatting | bytes 524288
Async XLA Ops:
  0.6 0.7 %copy-start.6 = (s32[2]{0:T(128)S(1)}, s32[2]{0:T(128)}, u32[]{:S(2)}) copy-start(s32[2]{0:T(128)} %owners.1) | copy-start | bytes 28
  0.6 0.7 %copy-start.7 = (s32[2]{0:T(128)S(1)}, s32[2]{0:T(128)}, u32[]{:S(2)}) copy-start(s32[2]{0:T(128)} %offsets.1) | copy-start | bytes 28
  1.3 1.2 %copy-start = (bf16[4,2,256,256]{3,2,1,0:T(8,128)(2,1)S(1)}, bf16[4,2,256,256]{3,2,1,0:T(8,128)(2,1)}, u32[]{:S(2)}) copy-start(bf16[4,2,256,256]{3,2,1,0:T(8,128)(2,1)} %constant.4.clone.matrices_hbm) | copy-start | bytes 3145732
  2.5 0.9 %copy-start.1 = (f32[32,2048]{1,0:T(8,128)S(1)}, f32[32,2048]{1,0:T(8,128)}, u32[]{:S(2)}) copy-start(f32[32,2048]{1,0:T(8,128)} %raw_re.1) | copy-start | bytes 786436
  3.5 0.9 %copy-start.2 = (f32[32,2048]{1,0:T(8,128)S(1)}, f32[32,2048]{1,0:T(8,128)}, u32[]{:S(2)}) copy-start(f32[32,2048]{1,0:T(8,128)} %raw_im.1) | copy-start | bytes 786436
  4.4 0.9 %copy-start.3 = (f32[2,128,128]{2,1,0:T(8,128)S(1)}, f32[2,128,128]{2,1,0:T(8,128)}, u32[]{:S(2)}) copy-start(f32[2,128,128]{2,1,0:T(8,128)} %constant.5.clone.twiddle_hbm) | copy-start | bytes 393220
  5.3 0.7 %copy-start.4 = (f32[1,64,32]{1,2,0:T(8,128)S(1)}, f32[1,64,32]{1,2,0:T(8,128)}, u32[]{:S(2)}) copy-start(f32[1,64,32]{1,2,0:T(8,128)} %param.10) | copy-start | bytes 24580
  6.1 0.7 %copy-start.5 = (f32[32,8]{0,1:T(8,128)S(1)}, f32[32,8]{0,1:T(8,128)}, u32[]{:S(2)}) copy-start(f32[32,8]{0,1:T(8,128)} %param.13) | copy-start | bytes 3076
where the time goes:
time: 42.8 us; the launch traced here: 42.4 us
  Pallas kernels  34.3 us (80%)
  local copies, waits for them, and re-layouts  7.49 us (18%)
  between operations  0.66 us (2%)
    pallas_call x1, Pallas kernels, fused_shards(): pl.pallas_call(functools.partial(focus_kernel, az_count), out_shape=[jax....  34.3 us
    unnamed x18, local copies, waits for them, and re-layouts  7.49 us

commit v1 on v0

--- a/solution.py
+++ b/solution.py
@@ -231,16 +231,19 @@
 
 def focus_kernel(
     az_count,
-    raw_re,
-    raw_im,
-    refs,
+    re_hbm,
+    im_hbm,
+    refs_hbm,
     owners,
     offsets,
-    taps,
+    taps_hbm,
     matrices_hbm,
     twiddle_hbm,
     out_re,
     out_im,
+    raw,
+    refs,
+    taps,
     matrices,
     twiddle,
     outgoing,
@@ -251,6 +254,7 @@
     focused,
     band,
     weigh,
+    raw_sem,
     const_sem,
     ref_send,
     ref_recv,
@@ -261,16 +265,35 @@
     rim_send,
     rim_recv,
 ):
-    rows = raw_re.shape[0]
-    inner = raw_re.shape[1] // LANES
+    rows = re_hbm.shape[0]
+    inner = re_hbm.shape[1] // LANES
     piece = 2 * inner
     steps = rows // az_count
     depth = band.shape[0] // piece
     me = lax.axis_index("az")
     core = lax.axis_index("rg")
-    peers = [lax.rem(me + s, az_count) for s in range(1, az_count)]
-    sources = [lax.rem(me + az_count - s, az_count) for s in range(1, az_count)]
+    peers = []
+    for flips in sorted(range(1, az_count), reverse=True):
+        peer = me
+        for bit in (1 << b for b in range(az_count.bit_length())):
+            if flips & bit:
+                peer = peer + bit - 2 * bit * lax.rem(lax.div(peer, bit), 2)
+        peers.append(peer)
+    sources = peers
     sibling = 1 - core
+    groups = [s + (1 - core) * (steps - 1 - 2 * s) for s in range(steps)]
+
+    def raw_copy(step, comp):
+        group = pl.ds(pl.multiple_of(groups[step] * az_count, az_count), az_count)
+        hbm = (re_hbm, im_hbm)[comp]
+        return pltpu.make_async_copy(hbm.at[group, :], raw.at[comp, step], raw_sem.at[step, comp])
+
+    load_refs = pltpu.make_async_copy(refs_hbm, refs, const_sem.at[2])
+    load_taps = pltpu.make_async_copy(taps_hbm, taps, const_sem.at[3])
+    load_refs.start()
+    for step in range(steps):
+        for comp in range(2):
+            raw_copy(step, comp).start()
 
     barrier = pltpu.get_barrier_semaphore()
     for peer in peers:
@@ -280,38 +303,22 @@
     load_twiddle = pltpu.make_async_copy(twiddle_hbm, twiddle, const_sem.at[1])
     load_matrices.start()
     load_twiddle.start()
-
-    groups = [s + (1 - core) * (steps - 1 - 2 * s) for s in range(steps)]
+    load_taps.start()
 
     def at(start, count):
         return pl.ds(start * piece if isinstance(start, int) else pl.multiple_of(start * piece, piece), count * piece)
 
-    for comp, raw in enumerate((raw_re, raw_im)):
-        for i in range(inner):
-            outgoing[pl.ds(comp * inner + i, rows, stride=piece), :] = raw[:, i * LANES : (i + 1) * LANES]
-
     ref_rows = refs.shape[1]
-    slot = lax.broadcasted_iota(jnp.int32, (depth, rows), 0)
-    target = lax.broadcasted_iota(jnp.int32, (depth, rows), 1)
-    target_block = target // BLOCK
-    for block in range(rows // BLOCK):
-        target = jnp.where(target_block == block, target + offsets[block], target)
-    weights = jnp.zeros((depth, rows), jnp.float32)
-    for tap in range(TAPS):
-        weights = weights + jnp.where(slot == target + (RIM + tap - TAPS // 2), taps[tap : tap + 1, :], 0.0)
-    high, low = split(weights.T)
-    weigh[...] = jnp.concatenate([high, high, low], axis=1)
     coarse = lax.broadcasted_iota(jnp.int32, (ref_rows, LANES), 0)
     column = lax.broadcasted_iota(jnp.int32, (ref_rows, LANES), 1)
     spread = (coarse == column // (LANES // ref_rows)).astype(jnp.float32)
+    load_refs.wait()
     wide = jnp.dot(refs[...], spread, precision=PRECISE, preferred_element_type=jnp.float32)
     ref_out[...] = jnp.zeros_like(ref_out)
     for dest in range(az_count):
         for group in range(steps):
             row = group * az_count + dest
             ref_out[dest, group : group + 1, :] = wide[row : row + 1, :]
-
-    pl.semaphore_wait(barrier, az_count)
 
     def ref_copy(s, peer, source):
         return pltpu.make_async_remote_copy(
@@ -368,15 +375,33 @@
             device_id_type=MESH,
         )
 
-    for s, peer in enumerate(peers):
-        ref_copy(s, peer, me).start()
     for step in range(steps):
+        for comp in range(2):
+            raw_copy(step, comp).wait()
+            for i in range(inner):
+                place = groups[step] * (az_count * piece) + (comp * inner + i)
+                outgoing[pl.ds(place, az_count, stride=piece), :] = raw[comp, step, :, i * LANES : (i + 1) * LANES]
+        if step == 0:
+            pl.semaphore_wait(barrier, az_count)
+            for s, peer in enumerate(peers):
+                ref_copy(s, peer, me).start()
         for s, peer in enumerate(peers):
             in_copy(step, s, peer, me).start()
-
-    for group in range(steps):
-        own = at(group * az_count + me, 1)
+        own = at(groups[step] * az_count + me, 1)
         incoming[own, :] = outgoing[own, :]
+
+    load_taps.wait()
+    slot = lax.broadcasted_iota(jnp.int32, (depth, rows), 0)
+    target = lax.broadcasted_iota(jnp.int32, (depth, rows), 1)
+    target_block = target // BLOCK
+    for block in range(rows // BLOCK):
+        target = jnp.where(target_block == block, target + offsets[block], target)
+    weights = jnp.zeros((depth, rows), jnp.float32)
+    for tap in range(TAPS):
+        weights = weights + jnp.where(slot == target + (RIM + tap - TAPS // 2), taps[tap : tap + 1, :], 0.0)
+    high, low = split(weights.T)
+    weigh[...] = jnp.concatenate([high, high, low], axis=1)
+
     ref_in[me] = ref_out[me]
     band[at((RIM + rows) * core, RIM), :] = jnp.zeros((RIM * piece, LANES), jnp.float32)
     spare = depth - rows - 2 * RIM
@@ -460,21 +485,25 @@
 
 def fused_shards(az_count, raw_re, raw_im, ref_blocks, owners, offsets, taps):
     rows, samples = raw_re.shape
+    ref_rows = ref_blocks.shape[1]
     piece = 2 * samples // LANES
     steps = rows // az_count
     depth = -(-(rows + 2 * RIM) // 16) * 16
     matrices, twiddle = tables(az_count)
     vmem = pl.BlockSpec(memory_space=pltpu.VMEM)
     smem = pl.BlockSpec(memory_space=pltpu.SMEM)
-    anywhere = pl.BlockSpec(memory_space=pl.ANY)
+    hbm = pl.BlockSpec(memory_space=pltpu.HBM)
     dma = pltpu.SemaphoreType.DMA
     flat = pltpu.VMEM((rows * piece, LANES), jnp.float32)
     return pl.pallas_call(
         functools.partial(focus_kernel, az_count),
         out_shape=[jax.ShapeDtypeStruct(raw_re.shape, jnp.float32)] * 2,
-        in_specs=[vmem, vmem, vmem, smem, smem, vmem, anywhere, anywhere],
+        in_specs=[hbm, hbm, hbm, smem, smem, hbm, hbm, hbm],
         out_specs=[vmem, vmem],
         scratch_shapes=[
+            pltpu.VMEM((2, steps, az_count, samples), jnp.float32),
+            pltpu.VMEM((rows, ref_rows), jnp.float32),
+            pltpu.VMEM((TAPS, rows), jnp.float32),
             pltpu.VMEM(matrices.shape, jnp.bfloat16),
             pltpu.VMEM(twiddle.shape, jnp.float32),
             flat,
@@ -485,7 +514,8 @@
             flat,
             pltpu.VMEM((depth * piece, LANES), jnp.float32),
             pltpu.VMEM((rows, 3 * depth), jnp.bfloat16),
-            dma((2,)),
+            dma((steps, 2)),
+            dma((4,)),
             dma((az_count,)),
             dma((az_count,)),
             dma((steps, az_count)),
@@ -496,7 +526,7 @@
             dma((2,)),
         ],
         compiler_params=pltpu.CompilerParams(
-            collective_id=0, has_side_effects=True, vmem_limit_bytes=32 * 1024 * 1024
+            collective_id=0, has_side_effects=True, vmem_limit_bytes=62 * 1024 * 1024
         ),
     )(raw_re, raw_im, ref_blocks[0].T, owners, offsets, taps.T, jnp.asarray(matrices), jnp.asarray(twiddle))
 

time: 42.8 us -> 38.1 us (0.89)
  local copies, waits for them, and re-layouts: 7.49 us -> 2.42 us
  Pallas kernels: 34.3 us -> 34.9 us
    unnamed x18 -> x4, local copies, waits for them, and re-layouts: 7.49 us -> 2.42 us
    pallas_call x1, Pallas kernels: 34.3 us -> 34.9 us  [fused_shards(): pl.pallas_call(functools.partial(focus_kernel, az_count), out_shape=[jax....]
where the time goes in v1:
time: 38.1 us; the launch traced here: 38 us
  Pallas kernels  34.9 us (92%)
  local copies, waits for them, and re-layouts  2.42 us (6%)
  between operations  0.65 us (2%)
    pallas_call x1, Pallas kernels, fused_shards(): pl.pallas_call(functools.partial(focus_kernel, az_count), out_shape=[jax....  34.9 us
    unnamed x4, local copies, waits for them, and re-layouts  2.42 us

profile of v1, /device:TPU:0, one launch (start us, length us, event | category | flops | bytes accessed | tf_op | source)
XLA Modules:
  0.0 38.0 jit_solution(173788690640036836)
XLA Ops:
  0.6 34.9 %shard_map.95 = (f32[32,2048]{1,0:T(8,128)}, f32[32,2048]{1,0:T(8,128)}) custom-call(f32[32,2048]{1,0:T(8,128)} %re_hbm.1, f32[32,2048]{1,0:T(8,128)} %im_hbm.1, f32[32,64]{1,0:T(8,128)} %bitcast.4, s32[2]{0:T(128)} %owners.1, s32[2]{0:T(128)} %offsets.1, f32[8,32]{1,0:T(8,128)} %bitcast.5, bf16[4,2,256,256]{3,2,1,0:T(8,128)(2,1)} %constant.4.clone.matrices_hbm, ...), custom_call_target="tpu_custom_call" | custom-call | tf_op jit(solution)/shard_map/pallas_call | solution.py:498
  35.5 0.0 copy-start
  35.6 1.7 %copy.12 = f32[32,2048]{1,0:T(8,128)} copy(f32[32,2048]{1,0:T(8,128)} %get-tuple-element.4) | data formatting | bytes 524288
  37.3 0.0 copy-done
  37.3 0.7 %copy.13 = f32[32,2048]{1,0:T(8,128)} copy(f32[32,2048]{1,0:T(8,128)S(1)} %copy-done) | data formatting | bytes 524288
Async XLA Ops:
  35.5 1.7 %copy-start = (f32[32,2048]{1,0:T(8,128)S(1)}, f32[32,2048]{1,0:T(8,128)}, u32[]{:S(2)}) copy-start(f32[32,2048]{1,0:T(8,128)} %get-tuple-element.5) | copy-start | bytes 786436

commit v2 on v1

--- a/solution.py
+++ b/solution.py
@@ -231,19 +231,16 @@
 
 def focus_kernel(
     az_count,
+    depth,
     re_hbm,
     im_hbm,
     refs_hbm,
     owners,
-    offsets,
-    taps_hbm,
     matrices_hbm,
     twiddle_hbm,
-    out_re,
-    out_im,
+    band,
     raw,
     refs,
-    taps,
     matrices,
     twiddle,
     outgoing,
@@ -252,10 +249,10 @@
     ref_in,
     filt,
     focused,
-    band,
-    weigh,
+    blank,
     raw_sem,
     const_sem,
+    own_sem,
     ref_send,
     ref_recv,
     in_send,
@@ -269,7 +266,6 @@
     inner = re_hbm.shape[1] // LANES
     piece = 2 * inner
     steps = rows // az_count
-    depth = band.shape[0] // piece
     me = lax.axis_index("az")
     core = lax.axis_index("rg")
     peers = []
@@ -289,7 +285,6 @@
         return pltpu.make_async_copy(hbm.at[group, :], raw.at[comp, step], raw_sem.at[step, comp])
 
     load_refs = pltpu.make_async_copy(refs_hbm, refs, const_sem.at[2])
-    load_taps = pltpu.make_async_copy(taps_hbm, taps, const_sem.at[3])
     load_refs.start()
     for step in range(steps):
         for comp in range(2):
@@ -303,7 +298,6 @@
     load_twiddle = pltpu.make_async_copy(twiddle_hbm, twiddle, const_sem.at[1])
     load_matrices.start()
     load_twiddle.start()
-    load_taps.start()
 
     def at(start, count):
         return pl.ds(start * piece if isinstance(start, int) else pl.multiple_of(start * piece, piece), count * piece)
@@ -349,6 +343,10 @@
             device_id={"az": peer},
             device_id_type=MESH,
         )
+
+    def own_copy(step):
+        row = groups[step] * az_count + me
+        return pltpu.make_async_copy(focused.at[at(row, 1), :], band.at[at(RIM + row, 1), :], own_sem.at[step])
 
     def rim_copy(step):
         count = (az_count, RIM - az_count)[step]
@@ -390,22 +388,15 @@
         own = at(groups[step] * az_count + me, 1)
         incoming[own, :] = outgoing[own, :]
 
-    load_taps.wait()
-    slot = lax.broadcasted_iota(jnp.int32, (depth, rows), 0)
-    target = lax.broadcasted_iota(jnp.int32, (depth, rows), 1)
-    target_block = target // BLOCK
-    for block in range(rows // BLOCK):
-        target = jnp.where(target_block == block, target + offsets[block], target)
-    weights = jnp.zeros((depth, rows), jnp.float32)
-    for tap in range(TAPS):
-        weights = weights + jnp.where(slot == target + (RIM + tap - TAPS // 2), taps[tap : tap + 1, :], 0.0)
-    high, low = split(weights.T)
-    weigh[...] = jnp.concatenate([high, high, low], axis=1)
-
     ref_in[me] = ref_out[me]
-    band[at((RIM + rows) * core, RIM), :] = jnp.zeros((RIM * piece, LANES), jnp.float32)
+    blank[...] = jnp.zeros_like(blank)
     spare = depth - rows - 2 * RIM
-    band[at(depth - spare, spare), :] = jnp.zeros((spare * piece, LANES), jnp.float32)
+    clear_rim = pltpu.make_async_copy(blank, band.at[at((RIM + rows) * core, RIM), :], const_sem.at[3])
+    clear_rim.start()
+    clear_spare = pltpu.make_async_copy(
+        blank.at[at(0, spare), :], band.at[at(depth - spare, spare), :], const_sem.at[4]
+    )
+    clear_spare.start()
 
     for s, source in enumerate(sources):
         ref_copy(s, peers[s], source).wait_recv()
@@ -451,28 +442,21 @@
         focused[whole, :] = left_apply((matrices[3, 0], matrices[3, 1]), value)
         for s, peer in enumerate(peers):
             back_copy(step, s, peer, me).start()
-        band[at(RIM + group * az_count + me, 1), :] = focused[at(group * az_count + me, 1), :]
+        own_copy(step).start()
         if step >= steps - 2:
             early = step - (steps - 2)
             for s, source in enumerate(sources):
                 back_copy(early, s, peers[s], source).wait_recv()
+            own_copy(early).wait()
             rim_copy(early).start()
+    clear_rim.wait()
+    clear_spare.wait()
     for step in range(2, steps):
+        own_copy(step).wait()
         for s, source in enumerate(sources):
             back_copy(step, s, peers[s], source).wait_recv()
     for step in range(2):
         rim_arrival(step).wait_recv()
-
-    weights = weigh[...]
-    pair = 2 * LANES
-    for comp, out in enumerate((out_re, out_im)):
-        for i in range(0, inner, 2):
-            value = jnp.concatenate(
-                [band[pl.ds(comp * inner + i + j, depth, stride=piece), :] for j in range(2)], axis=1
-            )
-            high, low = split(value)
-            value = dot(weights, jnp.concatenate([high, low, high], axis=0))
-            out[:, i * LANES : i * LANES + pair] = value
 
     for s, peer in enumerate(peers):
         ref_copy(s, peer, me).wait_send()
@@ -483,6 +467,51 @@
         rim_copy(step).wait_send()
 
 
+def stolt_kernel(piece, band_hbm, offsets, taps, out_re, out_im, band, image, in_sem, out_sem):
+    depth = band.shape[0] // piece
+    inner = piece // 2
+    half = inner // 2
+    rows = out_re.shape[0]
+    outs = (out_re, out_im)
+    loads = in_sem.shape[0]
+
+    def load(part):
+        lines = pl.ds(part * (band.shape[0] // loads), band.shape[0] // loads)
+        return pltpu.make_async_copy(band_hbm.at[lines, :], band.at[lines, :], in_sem.at[part])
+
+    def save(comp, part):
+        columns = pl.ds(part * half * LANES, half * LANES)
+        return pltpu.make_async_copy(image.at[comp, :, columns], outs[comp].at[:, columns], out_sem.at[comp, part])
+
+    for part in range(loads):
+        load(part).start()
+    slot = lax.broadcasted_iota(jnp.int32, (depth, rows), 0)
+    target = lax.broadcasted_iota(jnp.int32, (depth, rows), 1)
+    target_block = target // BLOCK
+    for block in range(rows // BLOCK):
+        target = jnp.where(target_block == block, target + offsets[block], target)
+    weights = jnp.zeros((depth, rows), jnp.float32)
+    for tap in range(TAPS):
+        weights = weights + jnp.where(slot == target + (RIM + tap - TAPS // 2), taps[tap : tap + 1, :], 0.0)
+    high, low = split(weights.T)
+    weights = jnp.concatenate([high, high, low], axis=1)
+    for part in range(loads):
+        load(part).wait()
+    for comp in range(2):
+        for part in range(2):
+            for i in range(part * half, part * half + half, 2):
+                value = jnp.concatenate(
+                    [band[pl.ds(comp * inner + i + j, depth, stride=piece), :] for j in range(2)], axis=1
+                )
+                high, low = split(value)
+                value = dot(weights, jnp.concatenate([high, low, high], axis=0))
+                image[comp, :, i * LANES : (i + 2) * LANES] = value
+            save(comp, part).start()
+    for comp in range(2):
+        for part in range(2):
+            save(comp, part).wait()
+
+
 def fused_shards(az_count, raw_re, raw_im, ref_blocks, owners, offsets, taps):
     rows, samples = raw_re.shape
     ref_rows = ref_blocks.shape[1]
@@ -490,20 +519,18 @@
     steps = rows // az_count
     depth = -(-(rows + 2 * RIM) // 16) * 16
     matrices, twiddle = tables(az_count)
-    vmem = pl.BlockSpec(memory_space=pltpu.VMEM)
     smem = pl.BlockSpec(memory_space=pltpu.SMEM)
-    hbm = pl.BlockSpec(memory_space=pltpu.HBM)
+    hbm = pl.BlockSpec(memory_space=pl.ANY)
     dma = pltpu.SemaphoreType.DMA
     flat = pltpu.VMEM((rows * piece, LANES), jnp.float32)
-    return pl.pallas_call(
-        functools.partial(focus_kernel, az_count),
-        out_shape=[jax.ShapeDtypeStruct(raw_re.shape, jnp.float32)] * 2,
-        in_specs=[hbm, hbm, hbm, smem, smem, hbm, hbm, hbm],
-        out_specs=[vmem, vmem],
+    band = pl.pallas_call(
+        functools.partial(focus_kernel, az_count, depth),
+        out_shape=jax.ShapeDtypeStruct((depth * piece, LANES), jnp.float32),
+        in_specs=[hbm, hbm, hbm, smem, hbm, hbm],
+        out_specs=hbm,
         scratch_shapes=[
             pltpu.VMEM((2, steps, az_count, samples), jnp.float32),
             pltpu.VMEM((rows, ref_rows), jnp.float32),
-            pltpu.VMEM((TAPS, rows), jnp.float32),
             pltpu.VMEM(matrices.shape, jnp.bfloat16),
             pltpu.VMEM(twiddle.shape, jnp.float32),
             flat,
@@ -512,10 +539,10 @@
             pltpu.VMEM((az_count, 8, LANES), jnp.float32),
             pltpu.VMEM((steps, 2, LANES, LANES), jnp.float32),
             flat,
-            pltpu.VMEM((depth * piece, LANES), jnp.float32),
-            pltpu.VMEM((rows, 3 * depth), jnp.bfloat16),
+            pltpu.VMEM((RIM * piece, LANES), jnp.float32),
             dma((steps, 2)),
-            dma((4,)),
+            dma((5,)),
+            dma((steps,)),
             dma((az_count,)),
             dma((az_count,)),
             dma((steps, az_count)),
@@ -528,7 +555,21 @@
         compiler_params=pltpu.CompilerParams(
             collective_id=0, has_side_effects=True, vmem_limit_bytes=62 * 1024 * 1024
         ),
-    )(raw_re, raw_im, ref_blocks[0].T, owners, offsets, taps.T, jnp.asarray(matrices), jnp.asarray(twiddle))
+    )(raw_re, raw_im, ref_blocks[0].T, owners, jnp.asarray(matrices), jnp.asarray(twiddle))
+    vmem = pl.BlockSpec(memory_space=pltpu.VMEM)
+    return pl.pallas_call(
+        functools.partial(stolt_kernel, piece),
+        out_shape=[jax.ShapeDtypeStruct(raw_re.shape, jnp.float32)] * 2,
+        in_specs=[hbm, smem, vmem],
+        out_specs=[hbm, hbm],
+        scratch_shapes=[
+            pltpu.VMEM((depth * piece, LANES), jnp.float32),
+            pltpu.VMEM((2, rows, samples), jnp.float32),
+            dma((4,)),
+            dma((2, 2)),
+        ],
+        compiler_params=pltpu.CompilerParams(vmem_limit_bytes=62 * 1024 * 1024),
+    )(band, offsets, taps.T)
 
 
 def body_for(mesh):

time: 38.1 us -> 37.9 us (level)
  local copies, waits for them, and re-layouts: 2.42 us -> 0 us
  Pallas kernels: 34.9 us -> 37 us
    unnamed x4 -> x0, local copies, waits for them, and re-layouts: 2.42 us -> none
    pallas_call x1 -> x2, Pallas kernels: 34.9 us -> 37 us  [the longest x1 33.6 us: fused_shards(): pl.pallas_call(functools.partial(focus_kernel, az_count, depth), out_shap...]
where the time goes in v2:
time: 37.9 us; the launch traced here: 37.6 us
  Pallas kernels  37 us (98%)
  between operations  0.64 us (2%)
    pallas_call x1, Pallas kernels, fused_shards(): pl.pallas_call(functools.partial(focus_kernel, az_count, depth), out_shap...  33.6 us
    pallas_call x1, Pallas kernels, fused_shards(): pl.pallas_call(functools.partial(stolt_kernel, piece), out_shape=[jax.Sha...  3.38 us

profile of v2, /device:TPU:0, one launch (start us, length us, event | category | flops | bytes accessed | tf_op | source)
XLA Modules:
  0.0 37.6 jit_solution(3580495108425189294)
XLA Ops:
  0.6 33.6 %shard_map.95.band_hbm = f32[2048,128]{1,0:T(8,128)} custom-call(f32[32,2048]{1,0:T(8,128)} %re_hbm.1, f32[32,2048]{1,0:T(8,128)} %im_hbm.1, f32[32,64]{1,0:T(8,128)} %bitcast.4, s32[2]{0:T(128)} %owners.1, bf16[4,2,256,256]{3,2,1,0:T(8,128)(2,1)} %constant.4.clone.matrices_hbm, f32[2,128,128]{2,1,0:T(8,128)} %constant.5.clone.twiddle_hbm), custom_call_target="tpu_custom_call" | custom-call | tf_op jit(solution)/shard_map/pallas_call | solution.py:526
  34.3 3.4 %shard_map.96 = (f32[32,2048]{1,0:T(8,128)}, f32[32,2048]{1,0:T(8,128)}) custom-call(f32[2048,128]{1,0:T(8,128)} %shard_map.95.band_hbm, s32[2]{0:T(128)} %offsets.1, f32[8,32]{1,0:T(8,128)} %bitcast.5), custom_call_target="tpu_custom_call" | custom-call | tf_op jit(solution)/shard_map/pallas_call | solution.py:560

commit v3 on v2

--- a/solution.py
+++ b/solution.py
@@ -250,6 +250,7 @@
     filt,
     focused,
     blank,
+    chosen,
     raw_sem,
     const_sem,
     own_sem,
@@ -277,10 +278,18 @@
         peers.append(peer)
     sources = peers
     sibling = 1 - core
-    groups = [s + (1 - core) * (steps - 1 - 2 * s) for s in range(steps)]
+    def group_of(step):
+        return step + (1 - core) * (steps - 1 - 2 * step)
+
+    def each(count, action):
+        def run(index, carry):
+            action(index)
+            return carry
+
+        lax.fori_loop(0, count, run, 0)
 
     def raw_copy(step, comp):
-        group = pl.ds(pl.multiple_of(groups[step] * az_count, az_count), az_count)
+        group = pl.ds(pl.multiple_of(group_of(step) * az_count, az_count), az_count)
         hbm = (re_hbm, im_hbm)[comp]
         return pltpu.make_async_copy(hbm.at[group, :], raw.at[comp, step], raw_sem.at[step, comp])
 
@@ -326,8 +335,8 @@
 
     def in_copy(step, s, peer, source):
         return pltpu.make_async_remote_copy(
-            src_ref=outgoing.at[at(groups[step] * az_count + peer, 1), :],
-            dst_ref=incoming.at[at(groups[step] * az_count + source, 1), :],
+            src_ref=outgoing.at[at(group_of(step) * az_count + peer, 1), :],
+            dst_ref=incoming.at[at(group_of(step) * az_count + source, 1), :],
             send_sem=in_send.at[step, s],
             recv_sem=in_recv.at[step, source],
             device_id={"az": peer},
@@ -336,8 +345,8 @@
 
     def back_copy(step, s, peer, source):
         return pltpu.make_async_remote_copy(
-            src_ref=focused.at[at(groups[step] * az_count + peer, 1), :],
-            dst_ref=band.at[at(RIM + groups[step] * az_count + source, 1), :],
+            src_ref=focused.at[at(group_of(step) * az_count + peer, 1), :],
+            dst_ref=band.at[at(RIM + group_of(step) * az_count + source, 1), :],
             send_sem=back_send.at[step, s],
             recv_sem=back_recv.at[step, source],
             device_id={"az": peer},
@@ -345,7 +354,7 @@
         )
 
     def own_copy(step):
-        row = groups[step] * az_count + me
+        row = group_of(step) * az_count + me
         return pltpu.make_async_copy(focused.at[at(row, 1), :], band.at[at(RIM + row, 1), :], own_sem.at[step])
 
     def rim_copy(step):
@@ -373,20 +382,22 @@
             device_id_type=MESH,
         )
 
-    for step in range(steps):
+    pl.semaphore_wait(barrier, az_count)
+    for s, peer in enumerate(peers):
+        ref_copy(s, peer, me).start()
+
+    def send(step):
         for comp in range(2):
             raw_copy(step, comp).wait()
             for i in range(inner):
-                place = groups[step] * (az_count * piece) + (comp * inner + i)
+                place = group_of(step) * (az_count * piece) + (comp * inner + i)
                 outgoing[pl.ds(place, az_count, stride=piece), :] = raw[comp, step, :, i * LANES : (i + 1) * LANES]
-        if step == 0:
-            pl.semaphore_wait(barrier, az_count)
-            for s, peer in enumerate(peers):
-                ref_copy(s, peer, me).start()
         for s, peer in enumerate(peers):
             in_copy(step, s, peer, me).start()
-        own = at(groups[step] * az_count + me, 1)
+        own = at(group_of(step) * az_count + me, 1)
         incoming[own, :] = outgoing[own, :]
+
+    each(steps, send)
 
     ref_in[me] = ref_out[me]
     blank[...] = jnp.zeros_like(blank)
@@ -405,6 +416,7 @@
     for source in range(az_count):
         wanted = jnp.where(lane < LANES // 2, owners[1], owners[0]) == source
         picked = jnp.where(wanted, ref_in[source], picked)
+    chosen[...] = picked
     az_total = LANES * LANES
     low = lax.broadcasted_iota(jnp.int32, (LANES, LANES), 0)
     high = lax.broadcasted_iota(jnp.int32, (LANES, LANES), 1)
@@ -412,18 +424,25 @@
     signed = jnp.where(frequency >= az_total // 2, frequency - az_total, frequency)
     az_freq = signed.astype(jnp.float32) / az_total
     az_square = az_freq * az_freq
-    for group in range(steps):
+    def make_filter(group):
         index = core * rows + group * az_count + me
         rg_freq = 1.0 + ((index.astype(jnp.float32) + 0.5) * (1.0 / (4 * rows)) - 0.25)
-        phase = PHASE_GAIN * jnp.sqrt(rg_freq * rg_freq - az_square) + picked[group : group + 1, :]
+        phase = PHASE_GAIN * jnp.sqrt(rg_freq * rg_freq - az_square) + chosen[pl.ds(group, 1), :]
         cosine, sine = cos_sin(phase)
         filt[group, 0] = cosine
         filt[group, 1] = sine
 
+    each(steps, make_filter)
+
     load_matrices.wait()
     load_twiddle.wait()
-    for step in range(steps):
-        group = groups[step]
+    def arrive(step):
+        own_copy(step).wait()
+        for s, source in enumerate(sources):
+            back_copy(step, s, peers[s], source).wait_recv()
+
+    def focus(step):
+        group = group_of(step)
         for s, source in enumerate(sources):
             in_copy(step, s, peers[s], source).wait_recv()
         whole = at(group * az_count, az_count)
@@ -443,26 +462,25 @@
         for s, peer in enumerate(peers):
             back_copy(step, s, peer, me).start()
         own_copy(step).start()
-        if step >= steps - 2:
-            early = step - (steps - 2)
-            for s, source in enumerate(sources):
-                back_copy(early, s, peers[s], source).wait_recv()
-            own_copy(early).wait()
-            rim_copy(early).start()
+
+    each(steps, focus)
+    for step in range(2):
+        arrive(step)
+        rim_copy(step).start()
     clear_rim.wait()
     clear_spare.wait()
-    for step in range(2, steps):
-        own_copy(step).wait()
-        for s, source in enumerate(sources):
-            back_copy(step, s, peers[s], source).wait_recv()
+    each(steps - 2, lambda step: arrive(step + 2))
     for step in range(2):
         rim_arrival(step).wait_recv()
 
+    def sent(step):
+        for s, peer in enumerate(peers):
+            in_copy(step, s, peer, me).wait_send()
+            back_copy(step, s, peer, me).wait_send()
+
+    each(steps, sent)
     for s, peer in enumerate(peers):
         ref_copy(s, peer, me).wait_send()
-        for step in range(steps):
-            in_copy(step, s, peer, me).wait_send()
-            back_copy(step, s, peer, me).wait_send()
     for step in range(2):
         rim_copy(step).wait_send()
 
@@ -540,6 +558,7 @@
             pltpu.VMEM((steps, 2, LANES, LANES), jnp.float32),
             flat,
             pltpu.VMEM((RIM * piece, LANES), jnp.float32),
+            pltpu.VMEM((8, LANES), jnp.float32),
             dma((steps, 2)),
             dma((5,)),
             dma((steps,)),

time: 37.9 us -> 36.8 us (0.971)
  Pallas kernels: 37 us -> 36 us
    pallas_call x1, Pallas kernels: 33.6 us -> 32.6 us  [fused_shards(): pl.pallas_call(functools.partial(focus_kernel, az_count, depth), out_shap...]
where the time goes in v3:
time: 36.8 us; the launch traced here: 36.6 us
  Pallas kernels  36 us (98%)
  between operations  0.64 us (2%)
    pallas_call x1, Pallas kernels, fused_shards(): pl.pallas_call(functools.partial(focus_kernel, az_count, depth), out_shap...  32.6 us
    pallas_call x1, Pallas kernels, fused_shards(): pl.pallas_call(functools.partial(stolt_kernel, piece), out_shape=[jax.Sha...  3.38 us

profile of v3, /device:TPU:0, one launch (start us, length us, event | category | flops | bytes accessed | tf_op | source)
XLA Modules:
  0.0 36.6 jit_solution(1964739488917942336)
XLA Ops:
  0.6 32.6 %shard_map.95.band_hbm = f32[2048,128]{1,0:T(8,128)} custom-call(f32[32,2048]{1,0:T(8,128)} %re_hbm.1, f32[32,2048]{1,0:T(8,128)} %im_hbm.1, f32[32,64]{1,0:T(8,128)} %bitcast.4, s32[2]{0:T(128)} %owners.1, bf16[4,2,256,256]{3,2,1,0:T(8,128)(2,1)} %constant.4.clone.matrices_hbm, f32[2,128,128]{2,1,0:T(8,128)} %constant.5.clone.twiddle_hbm), custom_call_target="tpu_custom_call" | custom-call | tf_op jit(solution)/shard_map/pallas_call | solution.py:544
  33.2 3.4 %shard_map.96 = (f32[32,2048]{1,0:T(8,128)}, f32[32,2048]{1,0:T(8,128)}) custom-call(f32[2048,128]{1,0:T(8,128)} %shard_map.95.band_hbm, s32[2]{0:T(128)} %offsets.1, f32[8,32]{1,0:T(8,128)} %bitcast.5), custom_call_target="tpu_custom_call" | custom-call | tf_op jit(solution)/shard_map/pallas_call | solution.py:579

commit v4 on v3

--- a/solution.py
+++ b/solution.py
@@ -382,21 +382,23 @@
             device_id_type=MESH,
         )
 
-    pl.semaphore_wait(barrier, az_count)
-    for s, peer in enumerate(peers):
-        ref_copy(s, peer, me).start()
-
-    def send(step):
+    def prepare(step):
         for comp in range(2):
             raw_copy(step, comp).wait()
             for i in range(inner):
                 place = group_of(step) * (az_count * piece) + (comp * inner + i)
                 outgoing[pl.ds(place, az_count, stride=piece), :] = raw[comp, step, :, i * LANES : (i + 1) * LANES]
+
+    def send(step):
         for s, peer in enumerate(peers):
             in_copy(step, s, peer, me).start()
         own = at(group_of(step) * az_count + me, 1)
         incoming[own, :] = outgoing[own, :]
 
+    each(steps, prepare)
+    pl.semaphore_wait(barrier, az_count)
+    for s, peer in enumerate(peers):
+        ref_copy(s, peer, me).start()
     each(steps, send)
 
     ref_in[me] = ref_out[me]

time: 36.8 us -> 36.8 us (level)
  no operation moved by 1% of the time
where the time goes in v4:
time: 36.8 us; the launch traced here: 36.6 us
  Pallas kernels  36 us (98%)
  between operations  0.64 us (2%)
    pallas_call x1, Pallas kernels, fused_shards(): pl.pallas_call(functools.partial(focus_kernel, az_count, depth), out_shap...  32.6 us
    pallas_call x1, Pallas kernels, fused_shards(): pl.pallas_call(functools.partial(stolt_kernel, piece), out_shape=[jax.Sha...  3.38 us

profile of v4, /device:TPU:0, one launch (start us, length us, event | category | flops | bytes accessed | tf_op | source)
XLA Modules:
  0.0 36.6 jit_solution(2004964817817737009)
XLA Ops:
  0.6 32.6 %shard_map.95.band_hbm = f32[2048,128]{1,0:T(8,128)} custom-call(f32[32,2048]{1,0:T(8,128)} %re_hbm.1, f32[32,2048]{1,0:T(8,128)} %im_hbm.1, f32[32,64]{1,0:T(8,128)} %bitcast.4, s32[2]{0:T(128)} %owners.1, bf16[4,2,256,256]{3,2,1,0:T(8,128)(2,1)} %constant.4.clone.matrices_hbm, f32[2,128,128]{2,1,0:T(8,128)} %constant.5.clone.twiddle_hbm), custom_call_target="tpu_custom_call" | custom-call | tf_op jit(solution)/shard_map/pallas_call | solution.py:546
  33.2 3.4 %shard_map.96 = (f32[32,2048]{1,0:T(8,128)}, f32[32,2048]{1,0:T(8,128)}) custom-call(f32[2048,128]{1,0:T(8,128)} %shard_map.95.band_hbm, s32[2]{0:T(128)} %offsets.1, f32[8,32]{1,0:T(8,128)} %bitcast.5), custom_call_target="tpu_custom_call" | custom-call | tf_op jit(solution)/shard_map/pallas_call | solution.py:581
